TPU v7x, 32 devices: a whole 2x2x4 slice. The times are simulated.
32 devices in a mesh: dp: 8 (over z, core), seq: 4 (over y, x).
Axes of the slice: x: 2, y: 2, z: 4, core: 2. Of those that a mesh axis runs over, the one named last changes fastest.
Arguments:
- queries: bfloat16 [8, 512, 4096], P('dp', 'seq'), may hold values from -6 to 6
- keys: bfloat16 [8, 512, 4096], P('dp', 'seq'), may hold values from -6 to 6
- values: bfloat16 [8, 512, 4096], P('dp', 'seq'), may hold values from -6 to 6
- cotangent: bfloat16 [8, 512, 4096], P('dp', 'seq'), may hold values from -6 to 6
- query_gain: float32 [32, 128], replicated, may hold values from 0.1 to 1.9
- key_gain: float32 [32, 128], replicated, may hold values from 0.1 to 1.9
- block_ids: int32 [8, 8], replicated, may hold values from -1 to 7, as said below
Outputs:
- out: bfloat16 [8, 512, 4096], P('dp', 'seq')
- query_grad: bfloat16 [8, 512, 4096], P('dp', 'seq')
- key_grad: bfloat16 [8, 512, 4096], P('dp', 'seq')
- value_grad: bfloat16 [8, 512, 4096], P('dp', 'seq')
- query_gain_grad: float32 [32, 128], replicated
- key_gain_grad: float32 [32, 128], replicated
Inputs may be any that keep to these rules, and one draw needn't show every extreme that they name: `block_ids`: every row block r lists block r, block 0 and block 7, two window slots for blocks r - 1 and r + 1 (set to -1 where such a block is missing or is block 0 or 7), and three further blocks; no block is listed twice in a row.
All inputs are finite; a program needn't handle non-finite values.
Results may differ from a plain program's by a relative error of at most 0.011.
Values may be sent and summed in bfloat16 or wider, within the bound.
A program may use at most 128 MiB of HBM per device.

v0:
```python
import functools

import jax
import jax.numpy as jnp
from jax import lax
from jax.experimental import pallas as pl
from jax.experimental.pallas import tpu as pltpu
from jax.sharding import PartitionSpec as P

BLOCK = 64
EPSILON = 1e-06
MESH = pl.DeviceIdType.MESH
F32 = jnp.float32
BF16 = jnp.bfloat16


def peer_of(me, step, n):
    if n & (n - 1):
        return lax.rem(me + step, n)
    other, bit = me, 1
    while bit < n:
        if step & bit:
            other = other + bit - 2 * bit * ((me // bit) % 2)
        bit *= 2
    return other


def dot(a, b, contract):
    return lax.dot_general(a, b, ((contract[:1], contract[1:]), ((), ())), preferred_element_type=F32)


def kernel(
    n, m, factor,
    q_in, k_in, v_in, g_in, q_gain, k_gain, ids,
    o_out, q_out, k_out, v_out, gains_out,
    held, made, mask, k_norm, k_sum, v_sum, part, slots, total,
    in_send, in_recv, out_send, out_recv, part_send, part_recv, gain_send, gain_recv,
):
    seq, dp = lax.axis_index("seq"), lax.axis_index("dp")
    count, tokens, width = q_in.shape
    units, _, length, depth = held.shape
    heads = units // count
    rows = min(length, max(BLOCK, 131072 // length))
    scale = depth ** (-0.5)
    ins, outs = (q_in, k_in, v_in, g_in), (o_out, q_out, k_out, v_out)

    barrier = pltpu.get_barrier_semaphore()
    for step in range(1, n):
        pl.semaphore_signal(barrier, inc=1, device_id={"seq": peer_of(seq, step, n)}, device_id_type=MESH)
    for step in range(1, m):
        pl.semaphore_signal(barrier, inc=1, device_id={"dp": peer_of(dp, step, m)}, device_id_type=MESH)

    column_block = lax.broadcasted_iota(jnp.int32, (BLOCK, length), 1) // BLOCK

    def mask_row(r, carry):
        found = column_block == ids[r, 0]
        for j in range(1, ids.shape[1]):
            found = found | (column_block == ids[r, j])
        mask[pl.ds(pl.multiple_of(r * BLOCK, BLOCK), BLOCK), :] = jnp.where(found, 1.0, 0.0)
        return carry

    part[...] = jnp.zeros_like(part)
    pl.semaphore_wait(barrier, n + m - 2)

    def columns(owner, hl):
        return pl.ds(pl.multiple_of((owner * heads + hl) * depth, depth), depth)

    def token_rows(owner):
        return pl.ds(pl.multiple_of(owner * tokens, tokens), tokens)

    def send_in(u, carry):
        c, hl = u // heads, u % heads
        for t in range(4):
            for step in range(1, n):
                peer = peer_of(seq, step, n)
                pltpu.make_async_remote_copy(
                    src_ref=ins[t].at[c, :, columns(peer, hl)],
                    dst_ref=held.at[u, t, token_rows(seq), :],
                    send_sem=in_send.at[t],
                    recv_sem=in_recv.at[u],
                    device_id={"seq": peer},
                    device_id_type=MESH,
                ).start()
            pltpu.make_async_copy(
                ins[t].at[c, :, columns(seq, hl)],
                held.at[u, t, token_rows(seq), :],
                in_recv.at[u],
            ).start()
        return carry

    lax.fori_loop(0, units, send_in, 0)
    lax.fori_loop(0, ids.shape[0], mask_row, 0)

    def normed(raw):
        inverse = lax.rsqrt(jnp.mean(raw * raw, axis=-1, keepdims=True) + EPSILON)
        return raw * inverse, inverse

    def raw_grad(grad, gain, hat, inverse):
        scaled = grad * gain
        return inverse * (scaled - hat * jnp.mean(scaled * hat, axis=-1, keepdims=True))

    def one_head(u, carry):
        c, hl = u // heads, u % heads
        pltpu.make_async_copy(held.at[u], held.at[u], in_recv.at[u]).wait()
        gain_row = pl.ds(seq * heads + hl, 1)
        gain_q, gain_k = q_gain[gain_row, :], k_gain[gain_row, :]
        k_hat, _ = normed(held[u, 1].astype(F32))
        k_norm[...] = (k_hat * gain_k).astype(BF16)
        k_sum[...] = jnp.zeros_like(k_sum)
        v_sum[...] = jnp.zeros_like(v_sum)

        def some_rows(i, gain_sum):
            at = pl.ds(pl.multiple_of(i * rows, rows), rows)
            q_hat, q_inverse = normed(held[u, 0, at, :].astype(F32))
            q_norm = (q_hat * gain_q).astype(BF16)
            grad = held[u, 3, at, :]
            scores = dot(q_norm, k_norm[...], (1, 1)) * scale
            raised = jnp.exp(scores) * mask[at, :]
            probs = raised * (1.0 / jnp.sum(raised, axis=-1, keepdims=True))
            weights = probs.astype(BF16)
            out = dot(weights, held[u, 2], (1, 0)).astype(BF16)
            made[u, 0, at, :] = out
            delta = jnp.sum(grad.astype(F32) * out.astype(F32), axis=-1, keepdims=True)
            grad_probs = dot(grad, held[u, 2], (1, 1))
            grad_scores = (probs * (grad_probs - delta)).astype(BF16)
            grad_qn = (dot(grad_scores, k_norm[...], (1, 0)) * scale).astype(BF16).astype(F32)
            made[u, 1, at, :] = raw_grad(grad_qn, gain_q, q_hat, q_inverse).astype(BF16)
            v_sum[...] += dot(weights, grad, (0, 0))
            k_sum[...] += dot(grad_scores, q_norm, (0, 0))
            return gain_sum + jnp.sum(grad_qn * q_hat, axis=0, keepdims=True)

        gain_sum = lax.fori_loop(0, length // rows, some_rows, jnp.zeros((1, depth), F32))
        grad_kn = (k_sum[...] * scale).astype(BF16).astype(F32)
        k_hat, k_inverse = normed(held[u, 1].astype(F32))
        made[u, 2] = raw_grad(grad_kn, gain_k, k_hat, k_inverse).astype(BF16)
        made[u, 3] = v_sum[...].astype(BF16)
        here = pl.ds(hl, 1)
        part[0, here, :] += gain_sum
        part[1, here, :] += jnp.sum(grad_kn * k_hat, axis=0, keepdims=True)
        for t in range(4):
            for step in range(1, n):
                peer = peer_of(seq, step, n)
                pltpu.make_async_remote_copy(
                    src_ref=made.at[u, t, token_rows(peer), :],
                    dst_ref=outs[t].at[c, :, columns(seq, hl)],
                    send_sem=out_send.at[t],
                    recv_sem=out_recv.at[t],
                    device_id={"seq": peer},
                    device_id_type=MESH,
                ).start()
            pltpu.make_async_copy(
                made.at[u, t, token_rows(seq), :],
                outs[t].at[c, :, columns(seq, hl)],
                out_recv.at[t],
            ).start()
        return carry

    lax.fori_loop(0, units, one_head, 0)

    for step in range(1, m):
        pltpu.make_async_remote_copy(
            src_ref=part,
            dst_ref=slots.at[dp],
            send_sem=part_send,
            recv_sem=part_recv,
            device_id={"dp": peer_of(dp, step, m)},
            device_id_type=MESH,
        ).start()
    pltpu.make_async_copy(part, slots.at[dp], part_recv).start()
    pltpu.make_async_copy(slots, slots, part_recv).wait()
    summed = slots[0]
    for j in range(1, m):
        summed = summed + slots[j]
    total[...] = summed * factor
    for step in range(1, n):
        pltpu.make_async_remote_copy(
            src_ref=total,
            dst_ref=gains_out.at[seq],
            send_sem=gain_send,
            recv_sem=gain_recv,
            device_id={"seq": peer_of(seq, step, n)},
            device_id_type=MESH,
        ).start()
    pltpu.make_async_copy(total, gains_out.at[seq], gain_recv).start()

    sent = pl.ds(0, (n - 1) * heads * depth)
    for t in range(4):
        away = ins[t].at[:, :, sent]
        pltpu.make_async_copy(away, away, in_send.at[t]).wait()
    for t in range(4):
        away = made.at[:, t, pl.ds(0, (n - 1) * tokens), :]
        pltpu.make_async_copy(away, away, out_send.at[t]).wait()
    others = slots.at[pl.ds(0, m - 1)]
    pltpu.make_async_copy(others, others, part_send).wait()
    others = gains_out.at[pl.ds(0, n - 1)]
    pltpu.make_async_copy(others, others, gain_send).wait()
    for t in range(4):
        pltpu.make_async_copy(outs[t], outs[t], out_recv.at[t]).wait()
    pltpu.make_async_copy(gains_out, gains_out, gain_recv).wait()


def on_device(n, m, queries, keys, values, cotangent, query_gain, key_gain, block_ids):
    count, tokens, width = queries.shape
    all_heads, depth = query_gain.shape
    heads, length = all_heads // n, tokens * n
    units = count * heads
    factor = (count * m * length) ** (-0.5)
    any_space = pl.BlockSpec(memory_space=pl.ANY)
    vmem = pl.BlockSpec(memory_space=pltpu.VMEM)
    block = jax.ShapeDtypeStruct(queries.shape, BF16)
    out, query_grad, key_grad, value_grad, gains = pl.pallas_call(
        functools.partial(kernel, n, m, factor),
        out_shape=(block,) * 4 + (jax.ShapeDtypeStruct((n, 2, heads, depth), F32),),
        in_specs=[any_space] * 4 + [vmem] * 2 + [pl.BlockSpec(memory_space=pltpu.SMEM)],
        out_specs=(any_space,) * 4 + (vmem,),
        scratch_shapes=[
            pltpu.VMEM((units, 4, length, depth), BF16),
            pltpu.VMEM((units, 4, length, depth), BF16),
            pltpu.VMEM((length, length), F32),
            pltpu.VMEM((length, depth), BF16),
            pltpu.VMEM((length, depth), F32),
            pltpu.VMEM((length, depth), F32),
            pltpu.VMEM((2, heads, depth), F32),
            pltpu.VMEM((m, 2, heads, depth), F32),
            pltpu.VMEM((2, heads, depth), F32),
            pltpu.SemaphoreType.DMA((4,)),
            pltpu.SemaphoreType.DMA((units,)),
            pltpu.SemaphoreType.DMA((4,)),
            pltpu.SemaphoreType.DMA((4,)),
            pltpu.SemaphoreType.DMA,
            pltpu.SemaphoreType.DMA,
            pltpu.SemaphoreType.DMA,
            pltpu.SemaphoreType.DMA,
        ],
        compiler_params=pltpu.CompilerParams(
            collective_id=0, has_side_effects=True, vmem_limit_bytes=60 * 1024 * 1024
        ),
        name="attention",
    )(queries, keys, values, cotangent, query_gain, key_gain, block_ids)
    return (
        out, query_grad, key_grad, value_grad,
        gains[:, 0].reshape(all_heads, depth),
        gains[:, 1].reshape(all_heads, depth),
    )


def solution(mesh):
    sharded, copied = P("dp", "seq", None), P()
    return jax.shard_map(
        functools.partial(on_device, mesh.shape["seq"], mesh.shape["dp"]),
        mesh=mesh,
        in_specs=(sharded,) * 4 + (copied,) * 3,
        out_specs=(sharded,) * 4 + (copied,) * 2,
        check_vma=False,
    )
```

profile of v0, /device:TPU:0, one launch (start us, length us, event | category | flops | bytes accessed | tf_op | source)
XLA Modules:
  0.0 109.3 jit_solution(8111084562221541946)
XLA Ops:
  0.6 100.8 %attention.1 = (bf16[1,128,4096]{2,1,0:T(8,128)(2,1)}, bf16[1,128,4096]{2,1,0:T(8,128)(2,1)}, bf16[1,128,4096]{2,1,0:T(8,128)(2,1)}, bf16[1,128,4096]{2,1,0:T(8,128)(2,1)}, f32[4,2,8,128]{3,2,1,0:T(8,128)}) custom-call(bf16[1,128,4096]{2,1,0:T(8,128)(2,1)} %q_in.1, bf16[1,128,4096]{2,1,0:T(8,128)(2,1)} %k_in.1, bf16[1,128,4096]{2,1,0:T(8,128)(2,1)} %v_in.1, ...), custom_call_target="tpu_custom_call" | custom-call | tf_op jit(solution)/shard_map/attention/pallas_call | solution.py:211
  101.4 1.3 %slice_bitcast_fusion = (f32[32,128]{1,0:T(8,128)}, f32[32,128]{1,0:T(8,128)}) fusion(f32[4,2,8,128]{3,2,1,0:T(8,128)} %get-tuple-element.15), kind=kLoop, calls=%fused_computation | loop fusion | bytes 65536 | tf_op jit(solution)/shard_map/reshape;squeeze | solution.py:243
  102.8 0.0 copy-start.2
  102.8 2.4 %copy.17 = bf16[1,128,4096]{2,1,0:T(8,128)(2,1)} copy(bf16[1,128,4096]{2,1,0:T(8,128)(2,1)} %get-tuple-element.24) | data formatting | bytes 2097152
  105.1 0.0 copy-done.2
  105.1 0.0 copy-start.1
  105.1 1.0 copy.18
  106.1 0.6 copy-done.1
  106.7 0.0 copy-start
  106.7 1.0 copy.19
  107.7 0.6 copy-done
  108.3 1.0 copy.20
Async XLA Ops:
  102.8 2.4 %copy-start.2 = (bf16[1,128,4096]{2,1,0:T(8,128)(2,1)S(1)}, bf16[1,128,4096]{2,1,0:T(8,128)(2,1)}, u32[]{:S(2)}) copy-start(bf16[1,128,4096]{2,1,0:T(8,128)(2,1)} %get-tuple-element.25) | copy-start | bytes 3145732
  105.1 1.6 %copy-start.1 = (bf16[1,128,4096]{2,1,0:T(8,128)(2,1)S(1)}, bf16[1,128,4096]{2,1,0:T(8,128)(2,1)}, u32[]{:S(2)}) copy-start(bf16[1,128,4096]{2,1,0:T(8,128)(2,1)} %get-tuple-element.26) | copy-start | bytes 3145732
  106.7 1.6 %copy-start = (bf16[1,128,4096]{2,1,0:T(8,128)(2,1)S(1)}, bf16[1,128,4096]{2,1,0:T(8,128)(2,1)}, u32[]{:S(2)}) copy-start(bf16[1,128,4096]{2,1,0:T(8,128)(2,1)} %get-tuple-element.27) | copy-start | bytes 3145732
where the time goes:
time: 110 us; the launch traced here: 109 us
  Pallas kernels  101 us (92%)
  local copies, waits for them, and re-layouts  7.9 us (7%)
    pallas_call x1, Pallas kernels, on_device(): pl.pallas_call(functools.partial(kernel, n, m, factor), out_shape=(block,...  101 us
    unnamed x10, local copies, waits for them, and re-layouts  6.55 us

commit v1 on v0

--- a/solution.py
+++ b/solution.py
@@ -9,6 +9,7 @@
 
 BLOCK = 64
 EPSILON = 1e-06
+VMEM_BYTES = 67043328
 MESH = pl.DeviceIdType.MESH
 F32 = jnp.float32
 BF16 = jnp.bfloat16
@@ -31,10 +32,10 @@
 
 def kernel(
     n, m, factor,
-    q_in, k_in, v_in, g_in, q_gain, k_gain, ids,
+    q_in, k_in, v_in, g_in, q_gain_in, k_gain_in, ids_in,
     o_out, q_out, k_out, v_out, gains_out,
     held, made, mask, k_norm, k_sum, v_sum, part, slots, total,
-    in_send, in_recv, out_send, out_recv, part_send, part_recv, gain_send, gain_recv,
+    q_gain, k_gain, ids, in_send, in_recv, out_send, out_recv, part_send, part_recv, gain_send, gain_recv, small,
 ):
     seq, dp = lax.axis_index("seq"), lax.axis_index("dp")
     count, tokens, width = q_in.shape
@@ -50,6 +51,12 @@
     for step in range(1, m):
         pl.semaphore_signal(barrier, inc=1, device_id={"dp": peer_of(dp, step, m)}, device_id_type=MESH)
 
+    small_copies = [
+        pltpu.make_async_copy(source, target, small.at[i])
+        for i, (source, target) in enumerate(((q_gain_in, q_gain), (k_gain_in, k_gain), (ids_in, ids)))
+    ]
+    for copy in small_copies:
+        copy.start()
     column_block = lax.broadcasted_iota(jnp.int32, (BLOCK, length), 1) // BLOCK
 
     def mask_row(r, carry):
@@ -89,6 +96,8 @@
         return carry
 
     lax.fori_loop(0, units, send_in, 0)
+    for copy in small_copies:
+        copy.wait()
     lax.fori_loop(0, ids.shape[0], mask_row, 0)
 
     def normed(raw):
@@ -199,20 +208,38 @@
     pltpu.make_async_copy(gains_out, gains_out, gain_recv).wait()
 
 
+def hand_over(o_in, q_in, k_in, v_in, gains_in, o_out, q_out, k_out, v_out, q_gain, k_gain, sems):
+    copies = [
+        pltpu.make_async_copy(source, target, sems.at[t])
+        for t, (source, target) in enumerate(
+            ((o_in, o_out), (q_in, q_out), (k_in, k_out), (v_in, v_out))
+        )
+    ]
+    for copy in copies:
+        copy.start()
+    heads = gains_in.shape[2]
+    for j in range(gains_in.shape[0]):
+        q_gain[j * heads : (j + 1) * heads, :] = gains_in[j, 0]
+        k_gain[j * heads : (j + 1) * heads, :] = gains_in[j, 1]
+    for copy in copies:
+        copy.wait()
+
+
 def on_device(n, m, queries, keys, values, cotangent, query_gain, key_gain, block_ids):
     count, tokens, width = queries.shape
     all_heads, depth = query_gain.shape
     heads, length = all_heads // n, tokens * n
     units = count * heads
     factor = (count * m * length) ** (-0.5)
-    any_space = pl.BlockSpec(memory_space=pl.ANY)
+    hbm = pl.BlockSpec(memory_space=pltpu.HBM)
     vmem = pl.BlockSpec(memory_space=pltpu.VMEM)
-    block = jax.ShapeDtypeStruct(queries.shape, BF16)
-    out, query_grad, key_grad, value_grad, gains = pl.pallas_call(
+    landing = pltpu.VMEM(queries.shape, BF16)
+    landed = 4 * queries.size * 2 + 2 * query_gain.size * 4
+    received = pl.pallas_call(
         functools.partial(kernel, n, m, factor),
-        out_shape=(block,) * 4 + (jax.ShapeDtypeStruct((n, 2, heads, depth), F32),),
-        in_specs=[any_space] * 4 + [vmem] * 2 + [pl.BlockSpec(memory_space=pltpu.SMEM)],
-        out_specs=(any_space,) * 4 + (vmem,),
+        out_shape=(landing,) * 4 + (pltpu.VMEM((n, 2, heads, depth), F32),),
+        in_specs=[hbm] * 7,
+        out_specs=(vmem,) * 5,
         scratch_shapes=[
             pltpu.VMEM((units, 4, length, depth), BF16),
             pltpu.VMEM((units, 4, length, depth), BF16),
@@ -223,6 +250,9 @@
             pltpu.VMEM((2, heads, depth), F32),
             pltpu.VMEM((m, 2, heads, depth), F32),
             pltpu.VMEM((2, heads, depth), F32),
+            pltpu.VMEM(query_gain.shape, F32),
+            pltpu.VMEM(key_gain.shape, F32),
+            pltpu.SMEM(block_ids.shape, jnp.int32),
             pltpu.SemaphoreType.DMA((4,)),
             pltpu.SemaphoreType.DMA((units,)),
             pltpu.SemaphoreType.DMA((4,)),
@@ -231,17 +261,24 @@
             pltpu.SemaphoreType.DMA,
             pltpu.SemaphoreType.DMA,
             pltpu.SemaphoreType.DMA,
+            pltpu.SemaphoreType.DMA((3,)),
         ],
         compiler_params=pltpu.CompilerParams(
-            collective_id=0, has_side_effects=True, vmem_limit_bytes=60 * 1024 * 1024
+            collective_id=0, has_side_effects=True, vmem_limit_bytes=VMEM_BYTES - landed - 524288
         ),
         name="attention",
     )(queries, keys, values, cotangent, query_gain, key_gain, block_ids)
-    return (
-        out, query_grad, key_grad, value_grad,
-        gains[:, 0].reshape(all_heads, depth),
-        gains[:, 1].reshape(all_heads, depth),
-    )
+    block = jax.ShapeDtypeStruct(queries.shape, BF16)
+    gain = jax.ShapeDtypeStruct(query_gain.shape, F32)
+    return pl.pallas_call(
+        hand_over,
+        out_shape=(block,) * 4 + (gain,) * 2,
+        in_specs=[vmem] * 5,
+        out_specs=(hbm,) * 4 + (vmem,) * 2,
+        scratch_shapes=[pltpu.SemaphoreType.DMA((4,))],
+        compiler_params=pltpu.CompilerParams(vmem_limit_bytes=16 * 1024 * 1024),
+        name="hand_over",
+    )(*received)
 
 
 def solution(mesh):

time: 110 us -> 103 us (0.936)
  local copies, waits for them, and re-layouts: 7.9 us -> 0 us
    unnamed x10 -> x0, local copies, waits for them, and re-layouts: 6.55 us -> none
    another operation x1 -> x0, local copies, waits for them, and re-layouts: 1.35 us -> none  [on_device(): gains[:, 1].reshape(all_heads, depth)]
    pallas_call x1 -> x2, Pallas kernels: 101 us -> 102 us  [the longest x1 99.3 us: on_device(): pl.pallas_call(functools.partial(kernel, n, m, factor), out_shape=(landin...]
where the time goes in v1:
time: 103 us
  Pallas kernels  102 us (99%)
    pallas_call x1, Pallas kernels, on_device(): pl.pallas_call(functools.partial(kernel, n, m, factor), out_shape=(landin...  99.3 us
    pallas_call x1, Pallas kernels, on_device(): pl.pallas_call(hand_over, out_shape=(block,) * 4 + (gain,) * 2, in_specs=...  2.65 us

profile of v1, /device:TPU:0, one launch (start us, length us, event | category | flops | bytes accessed | tf_op | source)
XLA Modules:
  0.0 102.6 jit_solution(16899273659186517369)
XLA Ops:
  0.6 99.3 %attention.1 = (bf16[1,128,4096]{2,1,0:T(8,128)(2,1)S(1)}, bf16[1,128,4096]{2,1,0:T(8,128)(2,1)S(1)}, bf16[1,128,4096]{2,1,0:T(8,128)(2,1)S(1)}, bf16[1,128,4096]{2,1,0:T(8,128)(2,1)S(1)}, f32[4,2,8,128]{3,2,1,0:T(8,128)S(1)}) custom-call(bf16[1,128,4096]{2,1,0:T(8,128)(2,1)} %q_in.1, bf16[1,128,4096]{2,1,0:T(8,128)(2,1)} %k_in.1, ...), custom_call_target="tpu_custom_call" | custom-call | tf_op jit(solution)/shard_map/attention/pallas_call | solution.py:238
  100.0 2.7 %hand_over.1 = (bf16[1,128,4096]{2,1,0:T(8,128)(2,1)}, bf16[1,128,4096]{2,1,0:T(8,128)(2,1)}, bf16[1,128,4096]{2,1,0:T(8,128)(2,1)}, bf16[1,128,4096]{2,1,0:T(8,...) custom-call(bf16[1,128,4096]{2,1,0:T(8,128)(2,1)S(1)} %get-tuple-element.11.o_in, ...), custom_call_target="tpu_custom_call" | custom-call | tf_op jit(solution)/shard_map/hand_over/pallas_call | solution.py:273

commit v2 on v1

--- a/solution.py
+++ b/solution.py
@@ -36,6 +36,7 @@
     o_out, q_out, k_out, v_out, gains_out,
     held, made, mask, k_norm, k_sum, v_sum, part, slots, total,
     q_gain, k_gain, ids, in_send, in_recv, out_send, out_recv, part_send, part_recv, gain_send, gain_recv, small,
+    ready, joined,
 ):
     seq, dp = lax.axis_index("seq"), lax.axis_index("dp")
     count, tokens, width = q_in.shape
@@ -46,10 +47,13 @@
     ins, outs = (q_in, k_in, v_in, g_in), (o_out, q_out, k_out, v_out)
 
     barrier = pltpu.get_barrier_semaphore()
+    gate = seq == 0
     for step in range(1, n):
-        pl.semaphore_signal(barrier, inc=1, device_id={"seq": peer_of(seq, step, n)}, device_id_type=MESH)
-    for step in range(1, m):
-        pl.semaphore_signal(barrier, inc=1, device_id={"dp": peer_of(dp, step, m)}, device_id_type=MESH)
+        peer = peer_of(seq, step, n)
+
+        @pl.when(peer != 0)
+        def _():
+            pl.semaphore_signal(barrier, inc=1, device_id={"seq": peer}, device_id_type=MESH)
 
     small_copies = [
         pltpu.make_async_copy(source, target, small.at[i])
@@ -67,7 +71,17 @@
         return carry
 
     part[...] = jnp.zeros_like(part)
-    pl.semaphore_wait(barrier, n + m - 2)
+
+    @pl.when(jnp.logical_not(gate))
+    def _():
+        pl.semaphore_wait(barrier, n - 1)
+        pl.semaphore_signal(ready, inc=1, device_id={"seq": 0}, device_id_type=MESH)
+
+    @pl.when(gate)
+    def _():
+        pl.semaphore_wait(ready, n - 1)
+        for step in range(1, m):
+            pl.semaphore_signal(barrier, inc=1, device_id={"dp": peer_of(dp, step, m)}, device_id_type=MESH)
 
     def columns(owner, hl):
         return pl.ds(pl.multiple_of((owner * heads + hl) * depth, depth), depth)
@@ -165,6 +179,16 @@
         return carry
 
     lax.fori_loop(0, units, one_head, 0)
+
+    @pl.when(gate)
+    def _():
+        pl.semaphore_wait(barrier, m - 1)
+        for step in range(1, n):
+            pl.semaphore_signal(joined, inc=1, device_id={"seq": step}, device_id_type=MESH)
+
+    @pl.when(jnp.logical_not(gate))
+    def _():
+        pl.semaphore_wait(joined, 1)
 
     for step in range(1, m):
         pltpu.make_async_remote_copy(
@@ -262,6 +286,8 @@
             pltpu.SemaphoreType.DMA,
             pltpu.SemaphoreType.DMA,
             pltpu.SemaphoreType.DMA((3,)),
+            pltpu.SemaphoreType.REGULAR,
+            pltpu.SemaphoreType.REGULAR,
         ],
         compiler_params=pltpu.CompilerParams(
             collective_id=0, has_side_effects=True, vmem_limit_bytes=VMEM_BYTES - landed - 524288

time: 103 us -> 99.1 us (0.962)
  Pallas kernels: 102 us -> 98.3 us
    pallas_call x1, Pallas kernels: 99.3 us -> 95.6 us  [on_device(): pl.pallas_call(functools.partial(kernel, n, m, factor), out_shape=(landin...]
where the time goes in v2:
time: 99.1 us; the launch traced here: 98.9 us
  Pallas kernels  98.3 us (99%)
    pallas_call x1, Pallas kernels, on_device(): pl.pallas_call(functools.partial(kernel, n, m, factor), out_shape=(landin...  95.6 us
    pallas_call x1, Pallas kernels, on_device(): pl.pallas_call(hand_over, out_shape=(block,) * 4 + (gain,) * 2, in_specs=...  2.65 us

profile of v2, /device:TPU:0, one launch (start us, length us, event | category | flops | bytes accessed | tf_op | source)
XLA Modules:
  0.0 98.9 jit_solution(3395821745485545672)
XLA Ops:
  0.6 95.6 %attention.1 = (bf16[1,128,4096]{2,1,0:T(8,128)(2,1)S(1)}, bf16[1,128,4096]{2,1,0:T(8,128)(2,1)S(1)}, bf16[1,128,4096]{2,1,0:T(8,128)(2,1)S(1)}, bf16[1,128,4096]{2,1,0:T(8,128)(2,1)S(1)}, f32[4,2,8,128]{3,2,1,0:T(8,128)S(1)}) custom-call(bf16[1,128,4096]{2,1,0:T(8,128)(2,1)} %q_in.1, bf16[1,128,4096]{2,1,0:T(8,128)(2,1)} %k_in.1, ...), custom_call_target="tpu_custom_call" | custom-call | tf_op jit(solution)/shard_map/attention/pallas_call | solution.py:262
  96.3 2.7 %hand_over.1 = (bf16[1,128,4096]{2,1,0:T(8,128)(2,1)}, bf16[1,128,4096]{2,1,0:T(8,128)(2,1)}, bf16[1,128,4096]{2,1,0:T(8,128)(2,1)}, bf16[1,128,4096]{2,1,0:T(8,...) custom-call(bf16[1,128,4096]{2,1,0:T(8,128)(2,1)S(1)} %get-tuple-element.11.o_in, ...), custom_call_target="tpu_custom_call" | custom-call | tf_op jit(solution)/shard_map/hand_over/pallas_call | solution.py:299
